TPU v7x, 32 devices: a whole 2x2x4 slice. The times are simulated.
32 devices in a mesh: groups: 2 (over x), depth: 16 (over z, y, core).
Axes of the slice: x: 2, y: 2, z: 4, core: 2. Of those that a mesh axis runs over, the one named last changes fastest.
Arguments:
- voxels: bfloat16 [256, 32, 16384], P(('groups', 'depth')), parts along dimension 0, may hold values from -6 to 6
- offsets: int32 [256], P('groups'), parts along dimension 0, may hold values from 0 to 127
- w_first: bfloat16 [64, 32], replicated, may hold values from -1 to 1
- decoder_second_weight: bfloat16 [33, 64], replicated, may hold values from -0.75 to 0.75
- cotangent: float32 [32, 32768], P(None, ('groups', 'depth')), parts along dimension 1, may hold values from -6 to 6
Outputs:
- image: float32 [32, 32768], P(None, ('groups', 'depth')), parts along dimension 1
- grad_voxels: bfloat16 [256, 32, 16384], P(('groups', 'depth')), parts along dimension 0
- grad_first: float32 [128, 32], P('groups'), parts along dimension 0
- grad_second: float32 [66, 64], P('groups'), parts along dimension 0
There are 2 independent parts, one for each index of `groups`. A program takes and returns all parts, laid end to end along the dimension named above; an argument that names none is the same for every part. Nothing has to cross between parts.
Inputs may be any that keep to these rules, and one draw needn't show every extreme that they name: offsets[p] counts tiles of 128 rays.
All inputs are finite; a program needn't handle non-finite values.
Results may differ from a plain program's by a relative error of at most 0.0085.
Values may be sent and summed in bfloat16 or wider, within the bound.
A program may use at most 192 MiB of HBM per device.

v0:
```python
import jax
import jax.numpy as jnp
from jax import lax
from jax.sharding import PartitionSpec as P

TILE = 128


def carried_in(x, axis, combine, identity):
    length, position = (lax.axis_size(axis), lax.axis_index(axis))
    everything = jax.tree.map(lambda part: lax.all_gather(part, axis), x)
    start = jax.tree.map(
        lambda part, zero: jnp.broadcast_to(jnp.asarray(zero, part.dtype), part.shape), x, identity
    )

    def step(k, before):
        reached = k < position
        new = combine(before, jax.tree.map(lambda part: part[k], everything))
        return jax.tree.map(lambda a, b: jnp.where(reached, a, b), new, before)

    return lax.fori_loop(0, length, step, start)


def decode_plane(plane, w_first, decoder_second_weight):
    preact = jnp.dot(w_first, plane, preferred_element_type=jnp.float32)
    hidden = jax.nn.silu(preact).astype(jnp.bfloat16)
    output_raw = jnp.dot(decoder_second_weight, hidden, preferred_element_type=jnp.float32)
    return (preact, hidden, output_raw)


def make_slab(output_raw, dscale):
    channels = output_raw.shape[0] - 1
    emitted_light = jax.nn.sigmoid(output_raw[:channels])
    density = jax.nn.softplus(output_raw[channels]) * dscale
    return jnp.concatenate([emitted_light, density[None]], 0).astype(jnp.bfloat16)


def move_rays(values, start):
    doubled = jnp.concatenate([values, values], values.ndim - 1)
    return lax.dynamic_slice_in_dim(doubled, start, values.shape[-1], values.ndim - 1)


def blended_image(slabs, upstream_gradient):
    channels = slabs.shape[1] - 1
    emitted_light = slabs[:, :channels].astype(jnp.float32)
    density = slabs[:, channels].astype(jnp.float32)
    passing = jnp.exp(-density)
    through = jnp.cumprod(passing, axis=0)
    before = jnp.concatenate([jnp.ones_like(through[:1]), through[:-1]], 0)
    sample_weight_rows = before * (1.0 - passing)
    pixel_colour = jnp.einsum("vi,vsi->si", sample_weight_rows, emitted_light)
    objective_value = jnp.einsum("vz,dvz->dz", upstream_gradient, emitted_light)
    running = jnp.cumsum(sample_weight_rows * objective_value, axis=0)
    return (
        passing,
        before,
        sample_weight_rows,
        objective_value,
        running,
        through[-1],
        pixel_colour,
    )


def slab_gradient(
    passing,
    before,
    sample_weight_rows,
    objective_value,
    running,
    upstream_gradient,
    enter,
    prior,
    ray_total,
):
    grad_rad = (enter * sample_weight_rows)[:, None, :] * upstream_gradient[None]
    grad_dens = enter * before * passing * objective_value - (ray_total - (prior + enter * running))
    return jnp.concatenate([grad_rad, grad_dens[:, None, :]], 1).astype(jnp.bfloat16)


def plane_backward(carry, inputs, w_first, decoder_second_weight, dscale):
    plane, grad_sheared, shift_tiles = inputs
    rays_count = plane.shape[1]
    preact, hidden, output_raw = decode_plane(plane, w_first, decoder_second_weight)
    grad_slab = move_rays(grad_sheared, rays_count - TILE * shift_tiles).astype(jnp.float32)
    channels = output_raw.shape[0] - 1
    sig_rad = jax.nn.sigmoid(output_raw[:channels])
    grad_rad = grad_slab[:channels] * sig_rad * (1.0 - sig_rad)
    grad_dens = grad_slab[channels] * dscale * jax.nn.sigmoid(output_raw[channels])
    grad_raw = jnp.concatenate([grad_rad, grad_dens[None]], 0).astype(jnp.bfloat16)
    grad_hidden = jnp.dot(decoder_second_weight.T, grad_raw, preferred_element_type=jnp.float32)
    sig_pre = jax.nn.sigmoid(preact)
    grad_pre = (grad_hidden * sig_pre * (1.0 + preact * (1.0 - sig_pre))).astype(jnp.bfloat16)
    grad_plane = jnp.dot(w_first.T, grad_pre, preferred_element_type=jnp.float32).astype(
        jnp.bfloat16
    )
    contract = (((1,), (1,)), ((), ()))
    acc_first = carry[0] + lax.dot_general(
        grad_pre, plane, contract, preferred_element_type=jnp.float32
    )
    acc_second = carry[1] + lax.dot_general(
        grad_raw, hidden, contract, preferred_element_type=jnp.float32
    )
    return ((acc_first, acc_second), grad_plane)


def join_depth(preceding_samples, later):
    return (preceding_samples[0] * later[0], preceding_samples[1] + preceding_samples[0] * later[1])


def shards(voxels, offsets, w_first, decoder_second_weight, cotangent):
    planes_here = voxels.shape[0]
    rays_count = voxels.shape[2]
    dscale = 3.0 / (planes_here * lax.axis_size("depth"))
    my_offsets = lax.dynamic_slice_in_dim(
        offsets, lax.axis_index("depth") * planes_here, planes_here
    )

    def forward_plane(inputs):
        plane, shift_tiles = inputs
        output_raw = decode_plane(plane, w_first, decoder_second_weight)[2]
        return move_rays(make_slab(output_raw, dscale), TILE * shift_tiles)

    slabs = lax.map(forward_plane, (voxels, my_offsets))
    cotan_full = lax.all_gather(cotangent, "depth", axis=1, tiled=True)
    passing, before, sample_weight_rows, objective_value, running, last_pass, pixel_colour = (
        blended_image(slabs, cotan_full)
    )
    identity = (jnp.ones((rays_count,), jnp.float32), jnp.zeros((rays_count,), jnp.float32))
    enter, prior = carried_in((last_pass, running[-1]), "depth", join_depth, identity)
    image = lax.psum_scatter(
        (enter[None, :] * pixel_colour).astype(jnp.bfloat16),
        "depth",
        scatter_dimension=1,
        tiled=True,
    ).astype(jnp.float32)
    ray_total = lax.psum(enter * running[-1], "depth")
    grad_sheared = slab_gradient(
        passing,
        before,
        sample_weight_rows,
        objective_value,
        running,
        cotan_full,
        enter,
        prior,
        ray_total,
    )

    def step_plane(carry, inputs):
        return plane_backward(carry, inputs, w_first, decoder_second_weight, dscale)

    start = (
        jnp.zeros(w_first.shape, jnp.float32),
        jnp.zeros(decoder_second_weight.shape, jnp.float32),
    )
    grads, grad_voxels = lax.scan(step_plane, start, (voxels, grad_sheared, my_offsets))
    grad_first, grad_second = lax.psum((grads[0], grads[1]), "depth")
    return (image, grad_voxels, grad_first, grad_second)


def solution(mesh):
    placed = (
        P(("groups", "depth"), None, None),
        P("groups"),
        P(),
        P(),
        P(None, ("groups", "depth")),
    )
    return jax.shard_map(
        shards,
        mesh=mesh,
        in_specs=placed,
        out_specs=(
            P(None, ("groups", "depth")),
            P(("groups", "depth"), None, None),
            P("groups", None),
            P("groups", None),
        ),
        check_vma=False,
    )
```

profile of v0, /device:TPU:0, one launch (start us, length us, event | category | flops | bytes accessed | tf_op | source)
XLA Modules:
  0.0 509.5 jit_solution(6826601035161955763)
XLA Ops:
  8.7 59.9 %while.43 = (s32[]{:T(128)}, bf16[8,33,16384]{2,1,0:T(8,128)(2,1)}, bf16[8,32,16384]{2,1,0:T(8,128)(2,1)}, bf16[64,32]{0,1:T(8,128)(2,1)}, bf16[33,64]{1,0:T(8,1...) while((s32[]{:T(128)}, bf16[8,33,16384]{2,1,0:T(8,128)(2,1)}, ...), condition=%wide.region_1.2_spmd, body=%wide.region_0.1_spmd.sunk | while | flops 148111360 | bytes 8865971 | solution.py:124
  9.9 3.1 convolution_bitcast_fusion.7
  17.4 3.1 convolution_bitcast_fusion.7
  54.8 3.1 convolution_bitcast_fusion.7
  62.3 3.1 convolution_bitcast_fusion.7
  68.6 12.2 %copy.12 = bf16[8,33,16384]{2,0,1:T(8,128)(2,1)} copy(bf16[8,33,16384]{2,1,0:T(8,128)(2,1)} %get-tuple-element.261) | data formatting | bytes 17301504 | tf_op jit(solution)/shard_map/while | solution.py:124
  83.3 6.6 %multiply_reduce_fusion.1 = f32[16384,8]{0,1:T(8,128)S(1)} fusion(f32[16384,32]{0,1:T(8,128)} %bitcast.152, bf16[8,33,16384]{2,1,0:T(8,128)(2,1)} %get-tuple-element.261), kind=kLoop, calls=%fused_computation.69 | loop fusion | flops 12451840 | bytes 11010048 | tf_op jit(solution)/shard_map/vz,dvz->dz/dot_general | solution.py:52
  92.2 31.6 %all-gather.8.cloned.1.call-done = f32[16,1,16384]{2,1,0:T(1,128)} async-done(((f32[1,1,16384]{2,1,0:T(1,128)}), f32[16,1,16384]{2,1,0:T(1,128)}) %all-gather.8.cloned.1.call-update) | async-done | bytes 1048592 | tf_op jit(solution)/shard_map/all_gather | solution.py:11
  125.6 37.8 %all-gather.10.cloned.1.call-done = f32[16,1,16384]{2,1,0:T(1,128)} async-done(((f32[1,1,16384]{2,1,0:T(1,128)}), f32[16,1,16384]{2,1,0:T(1,128)}) %all-gather.10.cloned.1.call-update) | async-done | bytes 1048592 | tf_op jit(solution)/shard_map/all_gather | solution.py:11
  166.2 19.4 %while.44 = (s32[]{:T(128)}, f32[16384]{0:T(1024)S(1)}, f32[16384]{0:T(1024)S(1)}, s32[]{:T(128)}, f32[16,16384]{1,0:T(8,128)S(1)}, /*index=5*/f32[16,16384]{1,0:T(8,128)}, s32[]{:T(128)}, s32[]{:T(128)}) while((s32[]{:T(128)}, f32[16384]{0:T(1024)S(1)}, f32[16384]{0:T(1024)S(1)}, s32[]{:T(128)}, f32[16,16384]{1,0:T(8,128)S(1)}, ...), condition=%wide.region_5.6_spmd.clone, body=%wide.region_4.5_spmd.clone.sunk | while | flops 114692 | bytes 655477 | solution.py:21
  186.3 85.3 %all-reduce.4.cloned.1.call-done = f32[16384]{0:T(1024)} async-done(((f32[16384]{0:T(1024)}), f32[16384]{0:T(1024)}) %all-reduce.4.cloned.1.call-update) | async-done | bytes 65552 | tf_op jit(solution)/shard_map/psum | solution.py:137
  272.8 5.4 %multiply_reduce_fusion = f32[16384,32]{0,1:T(8,128)S(1)} fusion(f32[16384,8]{0,1:T(8,128)S(1)} %get-tuple-element.370, bf16[8,33,16384]{2,1,0:T(8,128)(2,1)} %get-tuple-element.261), kind=kLoop, calls=%fused_computation.68 | loop fusion | flops 12058624 | bytes 11010048 | tf_op jit(solution)/shard_map/vi,vsi->si/dot_general | solution.py:51
  280.2 4.6 multiply_convert_fusion.2
  284.8 9.0 %pad_maximum_fusion.3 = bf16[8,33,16384]{2,1,0:T(8,128)(2,1)} fusion(bf16[8,1,16384]{2,1,0:T(2,128)(2,1)S(1)} %copy.13, bf16[8,32,16384]{2,1,0:T(8,128)(2,1)} %multiply_convert_fusion.2), kind=kLoop, calls=%fused_computation.71 | loop fusion | flops 17301504 | bytes 17301504 | tf_op jit(solution)/shard_map/concatenate | solution.py:78
  293.8 147.4 %while.45 = (s32[]{:T(128)}, f32[64,32]{0,1:T(8,128)S(1)}, f32[33,64]{1,0:T(8,128)S(1)}, bf16[8,32,16384]{2,1,0:T(8,128)(2,1)}, bf16[8,33,16384]{2,1,0:T(8,128)(...) while((s32[]{:T(128)}, f32[64,32]{0,1:T(8,128)S(1)}, ...), condition=%wide.region_9.10_spmd.clone, body=%wide.region_8.9_spmd.clone.sunk | while | flops 434413696 | bytes 81249400 | solution.py:157
  293.8 4.7 multiply_convert_fusion.5
  312.3 4.7 multiply_convert_fusion.5
  330.7 4.7 multiply_convert_fusion.5
  349.1 4.7 multiply_convert_fusion.5
  367.5 4.7 multiply_convert_fusion.5
  386.0 4.7 multiply_convert_fusion.5
  404.4 4.7 multiply_convert_fusion.5
  422.8 4.7 multiply_convert_fusion.5
  441.2 60.3 %all-reduce.1 = (f32[64,32]{0,1:T(8,128)}, f32[33,64]{1,0:T(8,128)}) all-reduce(f32[64,32]{0,1:T(8,128)S(1)} %get-tuple-element.265, f32[33,64]{1,0:T(8,128)S(1)} %get-tuple-element.266), channel_id=1, replica_groups=mesh['groups'=2,'depth'=16] {'depth'}, use_global_device_ids=true, to_apply=%region_10.11 | all-reduce | flops 4160 | bytes 33280 | tf_op jit(solution)/shard_map/psum | solution.py:158
  (266 shorter events, 180.8 us)
Async XLA Ops:
  7.2 76.1 %all-gather.6.cloned.1.call-start = ((), (), s32[]{:S(2)}) async-start(), calls=%async_computation.1 | async-start | bytes 2228224 | tf_op jit(solution)/shard_map/all_gather | solution.py:125
  7.9 115.9 %all-gather.8.cloned.1.call-start = ((), (), s32[]{:S(2)}) async-start(), calls=%async_computation.4 | async-start | bytes 1114112 | tf_op jit(solution)/shard_map/all_gather | solution.py:11
  83.0 80.4 %all-gather.10.cloned.1.call-start = ((), (), s32[]{:S(2)}) async-start(), calls=%async_computation.5 | async-start | bytes 1114112 | tf_op jit(solution)/shard_map/all_gather | solution.py:11
  92.1 179.5 %all-reduce.4.cloned.1.call-start = ((), (), s32[]{:S(2)}) async-start(), calls=%async_computation.3 | async-start | bytes 131072 | tf_op jit(solution)/shard_map/psum | solution.py:137
  186.2 315.2 %reduce-scatter.2.cloned.1.call-start = ((), (), s32[]{:S(2)}) async-start(), calls=%async_computation.2 | async-start | bytes 1114112 | tf_op jit(solution)/shard_map/reduce_scatter | solution.py:131
  284.8 9.1 %copy-start.5 = (bf16[33,64]{1,0:T(8,128)(2,1)S(1)}, bf16[33,64]{1,0:T(8,128)(2,1)}, u32[]{:S(2)}) copy-start(bf16[33,64]{1,0:T(8,128)(2,1)} %get-tuple-element.627) | copy-start | bytes 12676
  284.8 9.1 %copy-start.6 = (bf16[64,32]{0,1:T(8,128)(2,1)S(1)}, bf16[64,32]{0,1:T(8,128)(2,1)}, u32[]{:S(2)}) copy-start(bf16[64,32]{0,1:T(8,128)(2,1)} %get-tuple-element.628) | copy-start | bytes 12292
  303.6 2.2 copy-start.7
  307.9 2.1 copy-start.3
  307.9 2.2 copy-start.1
  322.0 2.2 copy-start.7
  326.3 2.2 copy-start.1
  340.5 2.2 copy-start.7
  344.7 2.2 copy-start.1
  358.9 2.2 copy-start.7
  363.2 2.2 copy-start.1
  377.3 2.2 copy-start.7
  381.6 2.2 copy-start.1
  395.7 2.2 copy-start.7
  400.0 2.2 copy-start.1
  414.1 2.2 copy-start.7
  418.4 2.2 copy-start.1
  432.5 2.2 copy-start.7
  436.8 2.2 copy-start.1
  (24 other events, 43.5 us)
Sparse Core Ops, SparseCore 0:
  10.2 44.1 all-gather.5
  83.1 40.6 all-gather.7
  126.5 36.8 all-gather.9
  186.3 85.2 all-reduce.3
  279.5 59.1 reduce-scatter.1
where the time goes:
time: 512 us; the launch traced here: 509 us
  waiting for transfers between devices  155 us (30%)
  matrix products  116 us (23%)
  local copies, waits for them, and re-layouts  79.1 us (15%)
  other arithmetic  72.1 us (14%)
  blocking collectives  60.3 us (12%)
  between operations  13.9 us (3%)
  loops' own time  12 us (2%)
    psum x1, waiting for transfers between devices, shards(): ray_total = lax.psum(enter * running[-1], 'depth')  85.3 us
    all_gather x2, waiting for transfers between devices, carried_in(): everything = jax.tree.map(lambda part: lax.all_gather(part, axis), x)  69.3 us
    psum x1, blocking collectives, shards(): grad_first, grad_second = lax.psum((grads[0], grads[1]), 'depth')  60.3 us
    dot_general x8, matrix products, decode_plane(): preact = jnp.dot(w_first, plane, preferred_element_type=jnp.float32)  37.7 us
    dot_general x16, matrix products, decode_plane(): jnp.dot(decoder_second_weight, hidden, preferred_element_type=jnp.float32)  28.6 us
    while x80, local copies, waits for them, and re-layouts  20.5 us
    dynamic_slice x16, local copies, waits for them, and re-layouts, step(): new = combine(before, jax.tree.map(lambda part: part[k], everything))  18.2 us
    dynamic_update_slice x8, other arithmetic, shards(): slabs = lax.map(forward_plane, (voxels, my_offsets))  18.2 us
  transfers between devices with their start and end apart: 5, of which 3 were waited for; matrix products, arithmetic and copies ran while one was open for 42% of the time, Pallas kernels for 0%

commit v1 on v0

--- a/solution.py
+++ b/solution.py
@@ -134,7 +134,7 @@
         scatter_dimension=1,
         tiled=True,
     ).astype(jnp.float32)
-    ray_total = lax.psum(enter * running[-1], "depth")
+    ray_total = jnp.sum(lax.all_gather(enter * running[-1], "depth"), axis=0)
     grad_sheared = slab_gradient(
         passing,
         before,

time: 512 us -> 466 us (0.910)
  waiting for transfers between devices: 155 us -> 107 us
    psum x1 -> x0, waiting for transfers between devices: 85.3 us -> none  [shards(): ray_total = lax.psum(enter * running[-1], 'depth')]
    all_gather x0 -> x1, waiting for transfers between devices: none -> 36.9 us  [shards(): ray_total = jnp.sum(lax.all_gather(enter * running[-1], 'depth'), axis=0)]
  transfers between devices with their start and end apart: 5 -> 5, of which waited for: 3 -> 3; matrix products, arithmetic and copies ran while one was open for 42% -> 46% of each run, Pallas kernels for 0% -> 0%
where the time goes in v1:
time: 466 us; the launch traced here: 463 us
  matrix products  116 us (25%)
  waiting for transfers between devices  107 us (23%)
  local copies, waits for them, and re-layouts  80.7 us (17%)
  other arithmetic  73.1 us (16%)
  blocking collectives  60 us (13%)
  between operations  13.9 us (3%)
  loops' own time  12 us (3%)
    all_gather x2, waiting for transfers between devices, carried_in(): everything = jax.tree.map(lambda part: lax.all_gather(part, axis), x)  69.3 us
    psum x1, blocking collectives, shards(): grad_first, grad_second = lax.psum((grads[0], grads[1]), 'depth')  60 us
    dot_general x8, matrix products, decode_plane(): preact = jnp.dot(w_first, plane, preferred_element_type=jnp.float32)  37.7 us
    all_gather x1, waiting for transfers between devices, shards(): ray_total = jnp.sum(lax.all_gather(enter * running[-1], 'depth'), axis=0)  36.9 us
    dot_general x16, matrix products, decode_plane(): jnp.dot(decoder_second_weight, hidden, preferred_element_type=jnp.float32)  28.5 us
    while x80, local copies, waits for them, and re-layouts  20.7 us
    dynamic_update_slice x8, other arithmetic, shards(): slabs = lax.map(forward_plane, (voxels, my_offsets))  18.2 us
    dynamic_slice x16, local copies, waits for them, and re-layouts, step(): new = combine(before, jax.tree.map(lambda part: part[k], everything))  18.2 us
  transfers between devices with their start and end apart: 5, of which 3 were waited for; matrix products, arithmetic and copies ran while one was open for 46% of the time, Pallas kernels for 0%

profile of v1, /device:TPU:0, one launch (start us, length us, event | category | flops | bytes accessed | tf_op | source)
XLA Modules:
  0.0 463.4 jit_solution(6832075475053844744)
XLA Ops:
  8.7 59.9 %while.43 = (s32[]{:T(128)}, bf16[8,33,16384]{2,1,0:T(8,128)(2,1)}, bf16[8,32,16384]{2,1,0:T(8,128)(2,1)}, bf16[64,32]{0,1:T(8,128)(2,1)}, bf16[33,64]{1,0:T(8,1...) while((s32[]{:T(128)}, bf16[8,33,16384]{2,1,0:T(8,128)(2,1)}, ...), condition=%wide.region_1.2_spmd, body=%wide.region_0.1_spmd.sunk | while | flops 148111360 | bytes 8865971 | solution.py:124
  9.9 3.1 convolution_bitcast_fusion.7
  17.4 3.1 convolution_bitcast_fusion.7
  32.4 3.1 convolution_bitcast_fusion.7
  39.8 3.1 convolution_bitcast_fusion.7
  68.6 12.2 %copy.14 = bf16[8,33,16384]{2,0,1:T(8,128)(2,1)} copy(bf16[8,33,16384]{2,1,0:T(8,128)(2,1)} %get-tuple-element.261) | data formatting | bytes 17301504 | tf_op jit(solution)/shard_map/while | solution.py:124
  83.3 6.6 %multiply_reduce_fusion.1 = f32[16384,8]{0,1:T(8,128)S(1)} fusion(f32[16384,32]{0,1:T(8,128)} %bitcast.152, bf16[8,33,16384]{2,1,0:T(8,128)(2,1)} %get-tuple-element.261), kind=kLoop, calls=%fused_computation.69 | loop fusion | flops 12451840 | bytes 11010048 | tf_op jit(solution)/shard_map/vz,dvz->dz/dot_general | solution.py:52
  92.2 31.5 %all-gather.12.cloned.1.call-done = f32[16,1,16384]{2,1,0:T(1,128)} async-done(((f32[1,1,16384]{2,1,0:T(1,128)}), f32[16,1,16384]{2,1,0:T(1,128)}) %all-gather.12.cloned.1.call-update) | async-done | bytes 1048592 | tf_op jit(solution)/shard_map/all_gather | solution.py:11
  125.6 37.8 %all-gather.14.cloned.1.call-done = f32[16,1,16384]{2,1,0:T(1,128)} async-done(((f32[1,1,16384]{2,1,0:T(1,128)}), f32[16,1,16384]{2,1,0:T(1,128)}) %all-gather.14.cloned.1.call-update) | async-done | bytes 1048592 | tf_op jit(solution)/shard_map/all_gather | solution.py:11
  166.2 19.4 %while.44 = (s32[]{:T(128)}, f32[16384]{0:T(1024)S(1)}, f32[16384]{0:T(1024)S(1)}, s32[]{:T(128)}, f32[16,16384]{1,0:T(8,128)S(1)}, /*index=5*/f32[16,16384]{1,0:T(8,128)}, s32[]{:T(128)}, s32[]{:T(128)}) while((s32[]{:T(128)}, f32[16384]{0:T(1024)S(1)}, f32[16384]{0:T(1024)S(1)}, s32[]{:T(128)}, f32[16,16384]{1,0:T(8,128)S(1)}, ...), condition=%wide.region_5.6_spmd.clone, body=%wide.region_4.5_spmd.clone.sunk | while | flops 114692 | bytes 655477 | solution.py:21
  186.3 36.9 %all-gather.10.cloned.1.call-done = f32[262144]{0:T(1024)} async-done(((f32[16384]{0:T(1024)}), f32[262144]{0:T(1024)}) %all-gather.10.cloned.1.call-update) | async-done | bytes 1048592 | tf_op jit(solution)/shard_map/all_gather | solution.py:137
  226.7 5.4 %multiply_reduce_fusion = f32[16384,32]{0,1:T(8,128)S(1)} fusion(f32[16384,8]{0,1:T(8,128)S(1)} %get-tuple-element.370, bf16[8,33,16384]{2,1,0:T(8,128)(2,1)} %get-tuple-element.261), kind=kLoop, calls=%fused_computation.68 | loop fusion | flops 12058624 | bytes 11010048 | tf_op jit(solution)/shard_map/vi,vsi->si/dot_general | solution.py:51
  234.2 4.6 multiply_convert_fusion.2
  238.8 9.1 %pad_maximum_fusion.3 = bf16[8,33,16384]{2,1,0:T(8,128)(2,1)} fusion(bf16[8,1,16384]{2,1,0:T(2,128)(2,1)S(1)} %copy.15, bf16[8,32,16384]{2,1,0:T(8,128)(2,1)} %multiply_convert_fusion.2), kind=kLoop, calls=%fused_computation.71 | loop fusion | flops 17301504 | bytes 17301504 | tf_op jit(solution)/shard_map/concatenate | solution.py:78
  247.9 147.4 %while.45 = (s32[]{:T(128)}, f32[64,32]{0,1:T(8,128)S(1)}, f32[33,64]{1,0:T(8,128)S(1)}, bf16[8,32,16384]{2,1,0:T(8,128)(2,1)}, bf16[8,33,16384]{2,1,0:T(8,128)(...) while((s32[]{:T(128)}, f32[64,32]{0,1:T(8,128)S(1)}, ...), condition=%wide.region_9.10_spmd.clone, body=%wide.region_8.9_spmd.clone.sunk | while | flops 434413696 | bytes 81249400 | solution.py:157
  247.9 4.7 %multiply_convert_fusion.5 = (bf16[64,16384]{1,0:T(8,128)(2,1)S(1)}, f32[64,16384]{1,0:T(8,128)}) fusion(bf16[64,32]{0,1:T(8,128)(2,1)S(1)} %get-tuple-element.603, bf16[8,32,16384]{2,1,0:T(8,128)(2,1)} %get-tuple-element.602, s32[]{:T(128)S(6)} %copy.57), kind=kOutput, calls=%fused_computation.37.clone.1 | convolution fusion | flops 72351744 | bytes 7344132 | tf_op jit(solution)/shard_map/while/body/eval_jaxpr/dot_general | solution.py:25
  266.4 4.7 %multiply_convert_fusion.5 = (bf16[64,16384]{1,0:T(8,128)(2,1)S(1)}, f32[64,16384]{1,0:T(8,128)}) fusion(bf16[64,32]{0,1:T(8,128)(2,1)S(1)} %get-tuple-element.603, bf16[8,32,16384]{2,1,0:T(8,128)(2,1)} %get-tuple-element.602, s32[]{:T(128)S(6)} %copy.57), kind=kOutput, calls=%fused_computation.37.clone.1 | convolution fusion | flops 72351744 | bytes 7344132 | tf_op jit(solution)/shard_map/while/body/eval_jaxpr/dot_general | solution.py:25
  284.9 4.7 %multiply_convert_fusion.5 = (bf16[64,16384]{1,0:T(8,128)(2,1)S(1)}, f32[64,16384]{1,0:T(8,128)}) fusion(bf16[64,32]{0,1:T(8,128)(2,1)S(1)} %get-tuple-element.603, bf16[8,32,16384]{2,1,0:T(8,128)(2,1)} %get-tuple-element.602, s32[]{:T(128)S(6)} %copy.57), kind=kOutput, calls=%fused_computation.37.clone.1 | convolution fusion | flops 72351744 | bytes 7344132 | tf_op jit(solution)/shard_map/while/body/eval_jaxpr/dot_general | solution.py:25
  303.3 4.7 %multiply_convert_fusion.5 = (bf16[64,16384]{1,0:T(8,128)(2,1)S(1)}, f32[64,16384]{1,0:T(8,128)}) fusion(bf16[64,32]{0,1:T(8,128)(2,1)S(1)} %get-tuple-element.603, bf16[8,32,16384]{2,1,0:T(8,128)(2,1)} %get-tuple-element.602, s32[]{:T(128)S(6)} %copy.57), kind=kOutput, calls=%fused_computation.37.clone.1 | convolution fusion | flops 72351744 | bytes 7344132 | tf_op jit(solution)/shard_map/while/body/eval_jaxpr/dot_general | solution.py:25
  321.7 4.7 %multiply_convert_fusion.5 = (bf16[64,16384]{1,0:T(8,128)(2,1)S(1)}, f32[64,16384]{1,0:T(8,128)}) fusion(bf16[64,32]{0,1:T(8,128)(2,1)S(1)} %get-tuple-element.603, bf16[8,32,16384]{2,1,0:T(8,128)(2,1)} %get-tuple-element.602, s32[]{:T(128)S(6)} %copy.57), kind=kOutput, calls=%fused_computation.37.clone.1 | convolution fusion | flops 72351744 | bytes 7344132 | tf_op jit(solution)/shard_map/while/body/eval_jaxpr/dot_general | solution.py:25
  340.1 4.7 %multiply_convert_fusion.5 = (bf16[64,16384]{1,0:T(8,128)(2,1)S(1)}, f32[64,16384]{1,0:T(8,128)}) fusion(bf16[64,32]{0,1:T(8,128)(2,1)S(1)} %get-tuple-element.603, bf16[8,32,16384]{2,1,0:T(8,128)(2,1)} %get-tuple-element.602, s32[]{:T(128)S(6)} %copy.57), kind=kOutput, calls=%fused_computation.37.clone.1 | convolution fusion | flops 72351744 | bytes 7344132 | tf_op jit(solution)/shard_map/while/body/eval_jaxpr/dot_general | solution.py:25
  358.5 4.7 %multiply_convert_fusion.5 = (bf16[64,16384]{1,0:T(8,128)(2,1)S(1)}, f32[64,16384]{1,0:T(8,128)}) fusion(bf16[64,32]{0,1:T(8,128)(2,1)S(1)} %get-tuple-element.603, bf16[8,32,16384]{2,1,0:T(8,128)(2,1)} %get-tuple-element.602, s32[]{:T(128)S(6)} %copy.57), kind=kOutput, calls=%fused_computation.37.clone.1 | convolution fusion | flops 72351744 | bytes 7344132 | tf_op jit(solution)/shard_map/while/body/eval_jaxpr/dot_general | solution.py:25
  376.9 4.7 %multiply_convert_fusion.5 = (bf16[64,16384]{1,0:T(8,128)(2,1)S(1)}, f32[64,16384]{1,0:T(8,128)}) fusion(bf16[64,32]{0,1:T(8,128)(2,1)S(1)} %get-tuple-element.603, bf16[8,32,16384]{2,1,0:T(8,128)(2,1)} %get-tuple-element.602, s32[]{:T(128)S(6)} %copy.57), kind=kOutput, calls=%fused_computation.37.clone.1 | convolution fusion | flops 72351744 | bytes 7344132 | tf_op jit(solution)/shard_map/while/body/eval_jaxpr/dot_general | solution.py:25
  395.3 60.0 %all-reduce.1 = (f32[64,32]{0,1:T(8,128)}, f32[33,64]{1,0:T(8,128)}) all-reduce(f32[64,32]{0,1:T(8,128)S(1)} %get-tuple-element.265, f32[33,64]{1,0:T(8,128)S(1)} %get-tuple-element.266), channel_id=1, replica_groups=mesh['groups'=2,'depth'=16] {'depth'}, use_global_device_ids=true, to_apply=%region_10.11 | all-reduce | flops 4160 | bytes 33280 | tf_op jit(solution)/shard_map/psum | solution.py:158
  (270 shorter events, 183.3 us)
Async XLA Ops:
  7.2 76.1 %all-gather.8.cloned.1.call-start = ((), (), s32[]{:S(2)}) async-start(), calls=%async_computation.1 | async-start | bytes 2228224 | tf_op jit(solution)/shard_map/all_gather | solution.py:125
  7.9 115.9 %all-gather.12.cloned.1.call-start = ((), (), s32[]{:S(2)}) async-start(), calls=%async_computation.4 | async-start | bytes 1114112 | tf_op jit(solution)/shard_map/all_gather | solution.py:11
  83.0 80.4 %all-gather.14.cloned.1.call-start = ((), (), s32[]{:S(2)}) async-start(), calls=%async_computation.5 | async-start | bytes 1114112 | tf_op jit(solution)/shard_map/all_gather | solution.py:11
  92.2 131.0 %all-gather.10.cloned.1.call-start = ((), (), s32[]{:S(2)}) async-start(), calls=%async_computation.3 | async-start | bytes 1114112 | tf_op jit(solution)/shard_map/all_gather | solution.py:137
  186.2 269.1 %reduce-scatter.2.cloned.1.call-start = ((), (), s32[]{:S(2)}) async-start(), calls=%async_computation.2 | async-start | bytes 1114112 | tf_op jit(solution)/shard_map/reduce_scatter | solution.py:131
  238.8 9.1 %copy-start.6 = (bf16[33,64]{1,0:T(8,128)(2,1)S(1)}, bf16[33,64]{1,0:T(8,128)(2,1)}, u32[]{:S(2)}) copy-start(bf16[33,64]{1,0:T(8,128)(2,1)} %get-tuple-element.628) | copy-start | bytes 12676
  238.8 9.1 %copy-start.7 = (bf16[64,32]{0,1:T(8,128)(2,1)S(1)}, bf16[64,32]{0,1:T(8,128)(2,1)}, u32[]{:S(2)}) copy-start(bf16[64,32]{0,1:T(8,128)(2,1)} %get-tuple-element.629) | copy-start | bytes 12292
  257.7 2.3 copy-start.8
  262.0 2.1 copy-start.3
  262.0 2.2 copy-start.1
  276.2 2.2 copy-start.8
  280.5 2.2 copy-start.1
  294.6 2.2 copy-start.8
  298.9 2.2 copy-start.1
  313.0 2.2 copy-start.8
  317.3 2.2 copy-start.1
  331.4 2.2 copy-start.8
  335.7 2.2 copy-start.1
  349.8 2.2 copy-start.8
  354.1 2.2 copy-start.1
  368.2 2.2 copy-start.8
  372.5 2.2 copy-start.1
  386.6 2.2 copy-start.8
  390.9 2.2 copy-start.1
  (25 other events, 44.7 us)
Sparse Core Ops, SparseCore 0:
  10.2 44.1 all-gather.7
  83.1 40.5 all-gather.11
  126.5 36.8 all-gather.13
  186.3 36.8 all-gather.9
  233.4 56.5 reduce-scatter.1
